TPU v7x, 256 devices: a whole 4x4x8 slice. The times are simulated.
256 devices in a mesh: tm: 32 (over y, x, core), space: 8 (over z).
Axes of the slice: x: 4, y: 4, z: 8, core: 2. Of those that a mesh axis runs over, the one named last changes fastest.
Arguments:
- latent_tokens: bfloat16 [64, 1792, 2240], P('tm', 'space'), may hold values from -6 to 6
- norm_gain: float32 [2240], replicated, may hold values from 0.5 to 1.5
- w_query: bfloat16 [2240, 1120], P('tm', 'space'), may hold values from -0.125 to 0.125
- w_key: bfloat16 [2240, 1120], P('tm', 'space'), may hold values from -0.125 to 0.125
- w_value: bfloat16 [2240, 1120], P('tm', 'space'), may hold values from -0.125 to 0.125
- out_gain: float32 [1120], replicated, may hold values from 0.5 to 1.5
- block_ids: int32 [64], P('tm'), may hold values from 0 to 15, never falling along the last dimension, each value on 1 to 8 neighbouring positions
Outputs:
- attended: bfloat16 [64, 1792, 1120], P('tm', 'space')
Inputs may be any that keep to these rules, and one draw needn't show every extreme that they name: `block_ids`: block numbers never fall from one frame to the next; each of the 16 blocks holds 1 to 8 frames and one holds exactly 8.
All inputs are finite; a program needn't handle non-finite values.
Results may differ from a plain program's by a relative error of at most 0.0065.
Values may be sent and summed in bfloat16 or wider, within the bound.
A program may use at most 192 MiB of HBM per device.

v0:
```python
import jax
import jax.numpy as jnp
from jax import lax
from jax.sharding import PartitionSpec as P

HEAD = 112
HEADS = 10


def gathered(weights):
    columns_full = lax.all_gather(jnp.stack(weights), "space", axis=2, tiled=True)
    return lax.all_gather(columns_full, "tm", axis=1, tiled=True)


def on_device(latent_tokens, norm_gain, w_query, w_key, w_value, out_gain, block_ids):
    frame_count, token_count, width = latent_tokens.shape
    row_count = frame_count * token_count
    values = latent_tokens.reshape(row_count, width).astype(jnp.float32)
    meansq = jnp.mean(values * values, axis=-1, keepdims=True)
    normed = (values * lax.rsqrt(meansq + 1e-06) * norm_gain).astype(jnp.bfloat16)
    pair = gathered((w_key, w_value))
    alone = gathered((w_query,))
    projected = jnp.einsum("rn,cnh->crh", normed, pair, preferred_element_type=jnp.float32)
    channels = projected.shape[2]
    headed = (frame_count, token_count, HEADS, HEAD)
    key = jax.nn.relu(projected[0]).astype(jnp.bfloat16).reshape(headed)
    value = projected[1].astype(jnp.bfloat16).reshape(headed)
    states = jnp.einsum("fthk,fthv->fhkv", key, value, preferred_element_type=jnp.float32)
    states = states.reshape(frame_count, channels, HEAD)
    mine = lax.psum_scatter(states, "space", scatter_dimension=1, tiled=True)
    everyone = lax.all_gather(mine.astype(jnp.bfloat16), "tm", tiled=True)
    all_ids = lax.all_gather(block_ids, "tm", tiled=True)
    reaches = (all_ids[None, :] <= block_ids[:, None]).astype(jnp.bfloat16)
    carried = jnp.einsum("fg,gkv->fkv", reaches, everyone, preferred_element_type=jnp.float32)
    carried = lax.all_gather(carried.astype(jnp.bfloat16), "space", axis=1, tiled=True)
    carried = carried.reshape(frame_count, HEADS, HEAD, HEAD)
    query = jnp.einsum("rn,cnh->crh", normed, alone, preferred_element_type=jnp.float32)[0]
    query = jax.nn.relu(query).astype(jnp.bfloat16).reshape(headed)
    numerator = jnp.einsum("fthk,fhkv->fthv", query, carried, preferred_element_type=jnp.float32)
    head_meansq = jnp.mean(numerator * numerator, axis=-1, keepdims=True)
    result = numerator * lax.rsqrt(head_meansq + 1e-06) * out_gain.reshape(HEADS, HEAD)
    return result.reshape(frame_count, token_count, channels).astype(jnp.bfloat16)


def solution(mesh):
    placed = (
        P("tm", "space", None),
        P(),
        P("tm", "space"),
        P("tm", "space"),
        P("tm", "space"),
        P(),
        P("tm"),
    )
    return jax.shard_map(
        on_device, mesh=mesh, in_specs=placed, out_specs=P("tm", "space", None), check_vma=False
    )
```

profile of v0, /device:TPU:6, one launch (start us, length us, event | category | flops | bytes accessed | tf_op | source)
XLA Modules:
  0.0 274.6 jit_solution(4759564278663120340)
XLA Ops:
  6.5 0.0 copy-start.3
  6.5 0.0 copy-start
  6.5 0.0 all-gather.8.cloned.1.call-start
  6.5 0.9 pad_maximum_fusion
  7.5 0.1 copy.40
  7.6 29.2 %all_gather.22 = bf16[2,70,1120]{1,0,2:T(2,128)(2,1)S(1)} all-gather(bf16[2,70,140]{1,0,2:T(2,128)(2,1)S(1)} %copy.40), channel_id=1, replica_groups=mesh['tm'=32,'space'=8] {'space'}, dimensions={2}, use_global_device_ids=true | all-gather | bytes 352800 | tf_op jit(solution)/shard_map/all_gather | solution.py:11
  36.9 2.2 copy.41
  39.0 0.0 copy-start.7
  39.0 0.0 copy-start.2
  39.0 0.0 all-gather.8.cloned.1.call-update
  39.1 0.0 all-gather.12.cloned.1.call-start
  39.1 0.0 copy-done.3
  39.1 0.1 copy.51
  39.2 25.1 %all-gather.2 = bf16[8,140,70]{2,1,0:T(8,128)(2,1)S(1)} all-gather(bf16[1,140,70]{2,1,0:T(8,128)(2,1)S(1)} %bitcast.50), channel_id=2, replica_groups=mesh['tm'=32,'space'=8] {'space'}, dimensions={0}, use_global_device_ids=true | all-gather | bytes 176400 | tf_op jit(solution)/shard_map/all_gather | solution.py:11
  64.3 0.1 reshape.90
  64.4 0.9 copy.65
  65.3 0.0 all-gather.12.cloned.1.call-update
  65.3 0.0 all-gather.10.cloned.1.call-start
  65.3 0.0 copy-done
  65.3 0.5 multiply_reduce_fusion
  65.8 0.1 rsqrt.21
  65.9 0.0 copy-done.7
  65.9 0.6 dynamic-slice.1
  67.1 0.0 copy-done.2
  67.1 1.8 fusion.3
  68.9 32.0 %all-gather.8.cloned.1.call-done = bf16[2,2240,1120]{2,0,1:T(2,128)(2,1)} async-done(((bf16[2,70,1120]{2,0,1:T(2,128)(2,1)}), bf16[2,2240,1120]{2,0,1:T(2,128)(2,1)}) %all-gather.8.cloned.1.call-update) | async-done | bytes 10035216 | tf_op jit(solution)/shard_map/all_gather | solution.py:12
  100.9 9.5 %fusion.4 = bf16[2,448,1120]{2,1,0:T(8,128)(2,1)S(1)} fusion(bf16[2,2240,1120]{2,0,1:T(2,128)(2,1)} %all-gather.8.cloned.1.call-done, bf16[448,2240]{1,0:T(8,128)(2,1)} %fusion.3), kind=kOutput, calls=%fused_computation.7 | convolution fusion | flops 4495769600 | bytes 14049280 | tf_op jit(solution)/shard_map/rn,cnh->crh/dot_general | solution.py:23
  110.4 1.2 fusion.14
  111.6 4.4 %reshape.88 = bf16[2,224,10,112]{3,2,1,0:T(8,128)(2,1)} reshape(bf16[1,448,1120]{2,1,0:T(8,128)(2,1)} %get-tuple-element.5) | data formatting | bytes 2007040 | tf_op jit(solution)/shard_map/convert_element_type | solution.py:26
  116.0 3.1 %reshape.89 = bf16[2,224,10,112]{3,2,1,0:T(8,128)(2,1)} reshape(bf16[1,448,1120]{2,1,0:T(8,128)(2,1)S(1)} %get-tuple-element.6) | data formatting | bytes 2007040 | tf_op jit(solution)/shard_map/convert_element_type | solution.py:27
  119.1 2.6 fusion.18
  121.8 0.0 copy-start.4
  121.8 0.0 copy-start.6
  121.8 0.0 copy-start.5
  121.8 4.2 %copy.47 = f32[2,1120,112]{2,0,1:T(2,128)S(1)} copy(f32[2,1120,112]{2,1,0:T(8,128)S(1)} %bitcast.46) | data formatting | bytes 2007040 | tf_op jit(solution)/shard_map/reshape | solution.py:29
  126.0 62.4 %all-reduce.3 = bf16[2,1120,112]{2,0,1:T(2,128)(2,1)} all-reduce(f32[2,1120,112]{2,0,1:T(2,128)S(1)} %copy.47), channel_id=4, replica_groups=mesh['tm'=32,'space'=8] {'space'}, use_global_device_ids=true, to_apply=%region_1.2.clone | all-reduce | flops 250880 | bytes 1505280
  188.4 0.9 dynamic-slice_convert_fusion
  189.3 0.6 copy.48
  190.0 0.0 all-gather.10.cloned.1.call-update
  190.0 0.0 copy-done.4
  190.0 0.1 mul.63
  190.1 0.0 copy-done.6
  190.1 0.6 dynamic-slice
  191.2 0.0 copy-done.5
  191.3 0.2 dynamic-update-slice
  191.5 14.1 %all-reduce = s32[64]{0:T(128)S(1)} all-reduce(s32[64]{0:T(128)S(1)} %dynamic-update-slice), channel_id=1, replica_groups=mesh['tm'=32,'space'=8] {'tm'}, use_global_device_ids=true, to_apply=%add | all-reduce | flops 64 | bytes 512
  205.6 1.9 multiply_convert_fusion
  207.5 0.0 copy-start.1
  207.5 0.0 all-gather.12.cloned.1.call-done
  207.5 8.1 %reshape.83 = bf16[2240,1120]{1,0:T(8,128)(2,1)} reshape(bf16[32,70,1120]{2,1,0:T(8,128)(2,1)} %all-gather.12.cloned.1.call-done) | data formatting | bytes 10035200
  215.6 0.0 copy-done.1
  215.6 5.3 %fusion.8 = bf16[1,448,1120]{2,1,0:T(8,128)(2,1)S(1)} fusion(bf16[448,2240]{1,0:T(8,128)(2,1)S(1)} %bitcast.48, bf16[2240,1120]{1,0:T(8,128)(2,1)} %reshape.83), kind=kOutput, calls=%fused_computation.10 | convolution fusion | flops 2248888320 | bytes 8028160 | tf_op jit(solution)/shard_map/rn,cnh->crh/dot_general | solution.py:37
  220.9 2.2 reshape.91
  223.1 13.1 %all-gather.10.cloned.1.call-done = bf16[64,140,112]{2,1,0:T(8,128)(2,1)} async-done(((bf16[2,140,112]{2,1,0:T(8,128)(2,1)}), bf16[64,140,112]{2,1,0:T(8,128)(2,1)}) %all-gather.10.cloned.1.call-update) | async-done | bytes 2007056 | tf_op jit(solution)/shard_map/all_gather | solution.py:31
  236.2 2.2 fusion.21
  238.4 27.0 %all_gather.25 = bf16[2,1120,112]{2,0,1:T(2,128)(2,1)S(1)} all-gather(bf16[2,140,112]{2,0,1:T(2,128)(2,1)S(1)} %fusion.21), channel_id=1, replica_groups=mesh['tm'=32,'space'=8] {'space'}, dimensions={1}, use_global_device_ids=true | all-gather | bytes 564480 | tf_op jit(solution)/shard_map/all_gather | solution.py:35
  265.4 0.9 fusion.9
  266.3 0.4 fusion.11
  266.7 1.4 copy.56
  (3 shorter events, 0.0 us)
Async XLA Ops:
  6.5 32.6 %copy-start.3 = (bf16[70,140]{1,0:T(8,128)(2,1)S(1)}, bf16[70,140]{1,0:T(8,128)(2,1)}, u32[]{:S(2)}) copy-start(bf16[70,140]{1,0:T(8,128)(2,1)} %param.9) | copy-start | bytes 58804
  6.5 58.8 %copy-start = (bf16[2,224,2240]{2,1,0:T(8,128)(2,1)S(1)}, bf16[2,224,2240]{2,1,0:T(8,128)(2,1)}, u32[]{:S(2)}) copy-start(bf16[2,224,2240]{2,1,0:T(8,128)(2,1)} %param.7) | copy-start | bytes 6021124
  6.5 94.4 %all-gather.8.cloned.1.call-start = ((), (), s32[]{:S(2)}) async-start(), calls=%async_computation | async-start | bytes 10644480 | tf_op jit(solution)/shard_map/all_gather | solution.py:12
  39.0 26.9 %copy-start.7 = (u32[256]{0:T(256)S(1)}, u32[256]{0:T(256)}, u32[]{:S(2)}) copy-start(u32[256]{0:T(256)} %constant.27) | copy-start | bytes 3076
  39.0 28.0 %copy-start.2 = (f32[2240]{0:T(1024)S(1)}, f32[2240]{0:T(1024)}, u32[]{:S(2)}) copy-start(f32[2240]{0:T(1024)} %param.8) | copy-start | bytes 26884
  39.1 168.4 %all-gather.12.cloned.1.call-start = ((), (), s32[]{:S(2)}) async-start(), calls=%async_computation.2 | async-start | bytes 5474304 | tf_op jit(solution)/shard_map/all_gather | solution.py:12
  65.3 170.9 %all-gather.10.cloned.1.call-start = ((), (), s32[]{:S(2)}) async-start(), calls=%async_computation.1 | async-start | bytes 2433024 | tf_op jit(solution)/shard_map/all_gather | solution.py:31
  121.8 68.2 %copy-start.4 = (f32[1120]{0:T(1024)S(1)}, f32[1120]{0:T(1024)}, u32[]{:S(2)}) copy-start(f32[1120]{0:T(1024)} %param.12) | copy-start | bytes 13444
  121.8 68.3 %copy-start.6 = (u32[256]{0:T(256)S(1)}, u32[256]{0:T(256)}, u32[]{:S(2)}) copy-start(u32[256]{0:T(256)} %constant.21) | copy-start | bytes 3076
  121.8 69.4 %copy-start.5 = (s32[2]{0:T(128)S(1)}, s32[2]{0:T(128)}, u32[]{:S(2)}) copy-start(s32[2]{0:T(128)} %param.13) | copy-start | bytes 28
  207.5 8.1 %copy-start.1 = (bf16[2,224,2240]{2,1,0:T(8,128)(2,1)S(1)}, bf16[2,224,2240]{2,1,0:T(8,128)(2,1)}, u32[]{:S(2)}) copy-start(bf16[2,224,2240]{2,1,0:T(8,128)(2,1)} %multiply_convert_fusion) | copy-start | bytes 6021124
Sparse Core Ops, SparseCore 0:
  39.2 61.6 all-gather.7
  103.5 51.7 all-gather.11
  190.1 46.0 all-gather.9
where the time goes:
time: 275 us
  blocking collectives  158 us (57%)
  waiting for transfers between devices  45.1 us (16%)
  local copies, waits for them, and re-layouts  29.9 us (11%)
  matrix products  20.5 us (7%)
  between operations  14.4 us (5%)
  other arithmetic  6.73 us (2%)
    unnamed x2, blocking collectives  76.5 us
    all_gather x2, blocking collectives, gathered(): lax.all_gather(jnp.stack(weights), 'space', axis=2, tiled=True)  54.3 us
    all_gather x2, waiting for transfers between devices, gathered(): return lax.all_gather(columns_full, 'tm', axis=1, tiled=True)  32 us
    all_gather x1, blocking collectives, on_device(): lax.all_gather(carried.astype(jnp.bfloat16), 'space', axis=1, tiled=True)  27 us
    all_gather x1, waiting for transfers between devices, on_device(): everyone = lax.all_gather(mine.astype(jnp.bfloat16), 'tm', tiled=True)  13.1 us
    unnamed x24, local copies, waits for them, and re-layouts  10.6 us
    dot_general x1, matrix products, on_device(): jnp.einsum('rn,cnh->crh', normed, pair, preferred_element_type=jnp.float32)  9.52 us
  transfers between devices with their start and end apart: 3, of which 2 were waited for; matrix products, arithmetic and copies ran while one was open for 18% of the time, Pallas kernels for 0%

commit v1 on v0

--- a/solution.py
+++ b/solution.py
@@ -7,8 +7,29 @@
 HEADS = 10
 
 
+def gather_around(shard, axis, dim):
+    length, index, rows = (lax.axis_size(axis), lax.axis_index(axis), shard.shape[dim])
+    right = [(i, (i + 1) % length) for i in range(length)]
+    backward = [(i, (i - 1) % length) for i in range(length)]
+    out = jnp.zeros((*shard.shape[:dim], length * rows, *shard.shape[dim + 1 :]), shard.dtype)
+    out = lax.dynamic_update_slice_in_dim(out, shard, index * rows, axis=dim)
+    from_left = from_right = shard
+    half = length // 2
+    for step in range(1, half + 1):
+        from_left = lax.ppermute(from_left, axis, right)
+        out = lax.dynamic_update_slice_in_dim(
+            out, from_left, (index - step) % length * rows, axis=dim
+        )
+        if step < length - half:
+            from_right = lax.ppermute(from_right, axis, backward)
+            out = lax.dynamic_update_slice_in_dim(
+                out, from_right, (index + step) % length * rows, axis=dim
+            )
+    return out
+
+
 def gathered(weights):
-    columns_full = lax.all_gather(jnp.stack(weights), "space", axis=2, tiled=True)
+    columns_full = gather_around(jnp.stack(weights), "space", 2)
     return lax.all_gather(columns_full, "tm", axis=1, tiled=True)
 
 

time: 275 us -> 420 us (1.53)
  local copies, waits for them, and re-layouts: 29.9 us -> 210 us
  blocking collectives: 158 us -> 104 us
  starting transfers between devices: 0.09 us -> 23.7 us
  waiting for transfers between devices: 45.1 us -> 33.2 us
    dynamic_update_slice x0 -> x16, local copies, waits for them, and re-layouts: none -> 189 us  [the longest x8 103 us: gather_around(): lax.dynamic_update_slice_in_dim(out, from_left, (index - step) % length *...]
    all_gather x2 -> x0, blocking collectives: 54.3 us -> none  [gathered(): lax.all_gather(jnp.stack(weights), 'space', axis=2, tiled=True)]
    all_gather x2, waiting for transfers between devices: 32 us -> 0.01 us  [gathered(): return lax.all_gather(columns_full, 'tm', axis=1, tiled=True)]
    ppermute x0 -> x14, starting transfers between devices: none -> 23.4 us  [the longest x6 20.8 us: gather_around(): from_right = lax.ppermute(from_right, axis, backward)]
    ppermute x0 -> x14, waiting for transfers between devices: none -> 12.2 us  [the longest x8 12.2 us: gather_around(): from_left = lax.ppermute(from_left, axis, right)]
    all_gather x1, waiting for transfers between devices: 13.1 us -> 21 us  [on_device(): everyone = lax.all_gather(mine.astype(jnp.bfloat16), 'tm', tiled=True)]
    unnamed x24 -> x22, local copies, waits for them, and re-layouts: 10.6 us -> 3.05 us
  transfers between devices with their start and end apart: 3 -> 17, of which waited for: 2 -> 7; matrix products, arithmetic and copies ran while one was open for 18% -> 53% of each run, Pallas kernels for 0% -> 0%
where the time goes in v1:
time: 420 us; the launch traced here: 416 us
  local copies, waits for them, and re-layouts  210 us (50%)
  blocking collectives  104 us (25%)
  waiting for transfers between devices  33.2 us (8%)
  starting transfers between devices  23.7 us (6%)
  matrix products  22.7 us (5%)
  between operations  15.4 us (4%)
  other arithmetic  6.54 us (2%)
    dynamic_update_slice x8, local copies, waits for them, and re-layouts, gather_around(): lax.dynamic_update_slice_in_dim(out, from_left, (index - step) % length *...  103 us
    dynamic_update_slice x6, local copies, waits for them, and re-layouts, gather_around(): lax.dynamic_update_slice_in_dim(out, from_right, (index + step) % length...  77.8 us
    unnamed x2, blocking collectives  76.9 us
    all_gather x1, blocking collectives, on_device(): lax.all_gather(carried.astype(jnp.bfloat16), 'space', axis=1, tiled=True)  27 us
    all_gather x1, waiting for transfers between devices, on_device(): everyone = lax.all_gather(mine.astype(jnp.bfloat16), 'tm', tiled=True)  21 us
    ppermute x6, starting transfers between devices, gather_around(): from_right = lax.ppermute(from_right, axis, backward)  20.8 us
    ppermute x8, waiting for transfers between devices, gather_around(): from_left = lax.ppermute(from_left, axis, right)  12.2 us
    dot_general x1, matrix products, on_device(): jnp.einsum('rn,cnh->crh', normed, pair, preferred_element_type=jnp.float32)  9.52 us
  transfers between devices with their start and end apart: 17, of which 7 were waited for; matrix products, arithmetic and copies ran while one was open for 53% of the time, Pallas kernels for 0%

profile of v1, /device:TPU:6, one launch (start us, length us, event | category | flops | bytes accessed | tf_op | source)
XLA Modules:
  0.0 415.9 jit_solution(3817728522846931052)
XLA Ops:
  6.5 0.8 pad_maximum_fusion
  7.4 2.0 collective-permute-start
  9.4 4.0 collective-permute-start.1
  13.4 2.2 collective-permute-done
  15.6 3.3 collective-permute-start.3
  18.9 2.2 collective-permute-done.2
  21.2 3.3 collective-permute-start.5
  24.5 2.2 collective-permute-done.4
  26.8 0.5 collective-permute-start.6
  27.5 0.2 broadcast_in_dim.4
  27.7 4.0 dynamic_update_slice.48
  31.8 12.8 %dynamic_update_slice.49 = bf16[2,70,1120]{2,0,1:T(2,128)(2,1)S(1)} dynamic-update-slice(bf16[2,70,1120]{2,0,1:T(2,128)(2,1)S(1)} %dynamic_update_slice.48, bf16[2,70,140]{2,0,1:T(2,128)(2,1)S(1)} %copy.35, s32[]{:T(128)} %constant.75.clone.1, s32[]{:T(128)} %constant.75.clone.1, s32[]{:T(128)S(6)} %select_n.79) | dynamic-update-slice | bytes 78404 | tf_op jit(solution)/shard_map/dynamic_update_slice | solution.py:20
  44.6 13.0 %dynamic_update_slice.50 = bf16[2,70,1120]{2,0,1:T(2,128)(2,1)S(1)} dynamic-update-slice(bf16[2,70,1120]{2,0,1:T(2,128)(2,1)S(1)} %dynamic_update_slice.49, bf16[2,70,140]{2,0,1:T(2,128)(2,1)S(1)} %copy.36, s32[]{:T(128)} %constant.75.clone.1, s32[]{:T(128)} %constant.75.clone.1, s32[]{:T(128)S(6)} %select_n.81) | dynamic-update-slice | bytes 78404 | tf_op jit(solution)/shard_map/dynamic_update_slice | solution.py:25
  57.6 13.0 %dynamic_update_slice.51 = bf16[2,70,1120]{2,0,1:T(2,128)(2,1)S(1)} dynamic-update-slice(bf16[2,70,1120]{2,0,1:T(2,128)(2,1)S(1)} %dynamic_update_slice.50, bf16[2,70,140]{2,0,1:T(2,128)(2,1)S(1)} %copy.37, s32[]{:T(128)} %constant.75.clone.1, s32[]{:T(128)} %constant.75.clone.1, s32[]{:T(128)S(6)} %select_n.83) | dynamic-update-slice | bytes 78404 | tf_op jit(solution)/shard_map/dynamic_update_slice | solution.py:20
  70.7 13.0 %dynamic_update_slice.52 = bf16[2,70,1120]{2,0,1:T(2,128)(2,1)S(1)} dynamic-update-slice(bf16[2,70,1120]{2,0,1:T(2,128)(2,1)S(1)} %dynamic_update_slice.51, bf16[2,70,140]{2,0,1:T(2,128)(2,1)S(1)} %copy.38, s32[]{:T(128)} %constant.75.clone.1, s32[]{:T(128)} %constant.75.clone.1, s32[]{:T(128)S(6)} %select_n.85) | dynamic-update-slice | bytes 78404 | tf_op jit(solution)/shard_map/dynamic_update_slice | solution.py:25
  83.7 13.0 %dynamic_update_slice.53 = bf16[2,70,1120]{2,0,1:T(2,128)(2,1)S(1)} dynamic-update-slice(bf16[2,70,1120]{2,0,1:T(2,128)(2,1)S(1)} %dynamic_update_slice.52, bf16[2,70,140]{2,0,1:T(2,128)(2,1)S(1)} %copy.39, s32[]{:T(128)} %constant.75.clone.1, s32[]{:T(128)} %constant.75.clone.1, s32[]{:T(128)S(6)} %select_n.87) | dynamic-update-slice | bytes 78404 | tf_op jit(solution)/shard_map/dynamic_update_slice | solution.py:20
  96.7 0.1 copy.40
  96.8 13.0 %dynamic_update_slice.54 = bf16[2,70,1120]{2,0,1:T(2,128)(2,1)S(1)} dynamic-update-slice(bf16[2,70,1120]{2,0,1:T(2,128)(2,1)S(1)} %dynamic_update_slice.53, bf16[2,70,140]{2,0,1:T(2,128)(2,1)S(1)} %copy.40, s32[]{:T(128)} %constant.75.clone.1, s32[]{:T(128)} %constant.75.clone.1, s32[]{:T(128)S(6)} %select_n.89) | dynamic-update-slice | bytes 78404 | tf_op jit(solution)/shard_map/dynamic_update_slice | solution.py:25
  109.8 13.0 %dynamic_update_slice.55 = bf16[2,70,1120]{2,0,1:T(2,128)(2,1)S(1)} dynamic-update-slice(bf16[2,70,1120]{2,0,1:T(2,128)(2,1)S(1)} %dynamic_update_slice.54, bf16[2,70,140]{2,0,1:T(2,128)(2,1)S(1)} %copy.41, s32[]{:T(128)} %constant.75.clone.1, s32[]{:T(128)} %constant.75.clone.1, s32[]{:T(128)S(6)} %select_n.91) | dynamic-update-slice | bytes 78404 | tf_op jit(solution)/shard_map/dynamic_update_slice | solution.py:20
  122.8 0.7 copy-done.2
  123.6 0.1 collective-permute-start.7
  123.7 3.3 collective-permute-start.8
  126.9 2.0 collective-permute-done.7
  128.9 3.4 collective-permute-start.10
  132.4 1.7 collective-permute-done.9
  134.1 3.4 collective-permute-start.12
  137.6 1.7 collective-permute-done.11
  139.3 0.2 broadcast_in_dim.5
  139.5 4.0 dynamic_update_slice.56
  143.7 12.8 %dynamic_update_slice.57 = bf16[1,70,1120]{2,0,1:T(2,128)(2,1)S(1)} dynamic-update-slice(bf16[1,70,1120]{2,0,1:T(2,128)(2,1)S(1)} %dynamic_update_slice.56, bf16[1,70,140]{2,0,1:T(2,128)(2,1)S(1)} %copy.52, s32[]{:T(128)} %constant.75.clone.1, s32[]{:T(128)} %constant.75.clone.1, s32[]{:T(128)S(6)} %select_n.79) | dynamic-update-slice | bytes 39204 | tf_op jit(solution)/shard_map/dynamic_update_slice | solution.py:20
  156.5 13.0 %dynamic_update_slice.58 = bf16[1,70,1120]{2,0,1:T(2,128)(2,1)S(1)} dynamic-update-slice(bf16[1,70,1120]{2,0,1:T(2,128)(2,1)S(1)} %dynamic_update_slice.57, bf16[1,70,140]{2,0,1:T(2,128)(2,1)S(1)} %copy.53, s32[]{:T(128)} %constant.75.clone.1, s32[]{:T(128)} %constant.75.clone.1, s32[]{:T(128)S(6)} %select_n.81) | dynamic-update-slice | bytes 39204 | tf_op jit(solution)/shard_map/dynamic_update_slice | solution.py:25
  169.5 13.0 %dynamic_update_slice.59 = bf16[1,70,1120]{2,0,1:T(2,128)(2,1)S(1)} dynamic-update-slice(bf16[1,70,1120]{2,0,1:T(2,128)(2,1)S(1)} %dynamic_update_slice.58, bf16[1,70,140]{2,0,1:T(2,128)(2,1)S(1)} %copy.54, s32[]{:T(128)} %constant.75.clone.1, s32[]{:T(128)} %constant.75.clone.1, s32[]{:T(128)S(6)} %select_n.83) | dynamic-update-slice | bytes 39204 | tf_op jit(solution)/shard_map/dynamic_update_slice | solution.py:20
  182.6 13.0 %dynamic_update_slice.60 = bf16[1,70,1120]{2,0,1:T(2,128)(2,1)S(1)} dynamic-update-slice(bf16[1,70,1120]{2,0,1:T(2,128)(2,1)S(1)} %dynamic_update_slice.59, bf16[1,70,140]{2,0,1:T(2,128)(2,1)S(1)} %copy.55, s32[]{:T(128)} %constant.75.clone.1, s32[]{:T(128)} %constant.75.clone.1, s32[]{:T(128)S(6)} %select_n.85) | dynamic-update-slice | bytes 39204 | tf_op jit(solution)/shard_map/dynamic_update_slice | solution.py:25
  195.6 13.0 %dynamic_update_slice.61 = bf16[1,70,1120]{2,0,1:T(2,128)(2,1)S(1)} dynamic-update-slice(bf16[1,70,1120]{2,0,1:T(2,128)(2,1)S(1)} %dynamic_update_slice.60, bf16[1,70,140]{2,0,1:T(2,128)(2,1)S(1)} %copy.56, s32[]{:T(128)} %constant.75.clone.1, s32[]{:T(128)} %constant.75.clone.1, s32[]{:T(128)S(6)} %select_n.87) | dynamic-update-slice | bytes 39204 | tf_op jit(solution)/shard_map/dynamic_update_slice | solution.py:20
  208.6 13.0 %dynamic_update_slice.62 = bf16[1,70,1120]{2,0,1:T(2,128)(2,1)S(1)} dynamic-update-slice(bf16[1,70,1120]{2,0,1:T(2,128)(2,1)S(1)} %dynamic_update_slice.61, bf16[1,70,140]{2,0,1:T(2,128)(2,1)S(1)} %copy.57, s32[]{:T(128)} %constant.75.clone.1, s32[]{:T(128)} %constant.75.clone.1, s32[]{:T(128)S(6)} %select_n.89) | dynamic-update-slice | bytes 39204 | tf_op jit(solution)/shard_map/dynamic_update_slice | solution.py:25
  221.7 13.0 %dynamic_update_slice.63 = bf16[1,70,1120]{2,0,1:T(2,128)(2,1)S(1)} dynamic-update-slice(bf16[1,70,1120]{2,0,1:T(2,128)(2,1)S(1)} %dynamic_update_slice.62, bf16[1,70,140]{2,0,1:T(2,128)(2,1)S(1)} %copy.58, s32[]{:T(128)} %constant.75.clone.1, s32[]{:T(128)} %constant.75.clone.1, s32[]{:T(128)S(6)} %select_n.91) | dynamic-update-slice | bytes 39204 | tf_op jit(solution)/shard_map/dynamic_update_slice | solution.py:20
  234.7 0.7 copy-done.1
  235.4 0.3 all-gather.6.cloned.1.call-start
  235.7 0.5 multiply_reduce_fusion
  236.2 0.1 rsqrt.21
  236.3 0.7 dynamic-slice.1
  237.6 1.9 fusion.6
  239.5 9.5 %fusion.7 = bf16[2,448,1120]{2,1,0:T(8,128)(2,1)S(1)} fusion(bf16[2,2240,1120]{2,0,1:T(2,128)(2,1)} %all-gather.4.cloned.1.call-done, bf16[448,2240]{1,0:T(8,128)(2,1)} %fusion.6), kind=kOutput, calls=%fused_computation.10 | convolution fusion | flops 4495769600 | bytes 14049280 | tf_op jit(solution)/shard_map/rn,cnh->crh/dot_general | solution.py:44
  249.0 1.2 fusion.24
  250.2 4.5 %reshape.81 = bf16[2,224,10,112]{3,2,1,0:T(8,128)(2,1)} reshape(bf16[1,448,1120]{2,1,0:T(8,128)(2,1)} %get-tuple-element.5) | data formatting | bytes 2007040 | tf_op jit(solution)/shard_map/convert_element_type | solution.py:47
  254.6 3.1 reshape.82
  257.7 2.7 fusion.28
  260.4 4.2 %copy.47 = f32[2,1120,112]{2,0,1:T(2,128)S(1)} copy(f32[2,1120,112]{2,1,0:T(8,128)S(1)} %bitcast.47) | data formatting | bytes 2007040 | tf_op jit(solution)/shard_map/reshape | solution.py:50
  264.6 61.9 %all-reduce.3 = bf16[2,1120,112]{2,0,1:T(2,128)(2,1)} all-reduce(f32[2,1120,112]{2,0,1:T(2,128)S(1)} %copy.47), channel_id=2, replica_groups=mesh['tm'=32,'space'=8] {'space'}, use_global_device_ids=true, to_apply=%region_1.2.clone | all-reduce | flops 250880 | bytes 1505280
  326.5 0.9 dynamic-slice_convert_fusion
  327.4 0.6 copy.48
  328.1 0.1 mul.103
  328.2 0.7 dynamic-slice
  329.5 0.2 dynamic-update-slice
  329.8 15.0 %all-reduce = s32[64]{0:T(128)S(1)} all-reduce(s32[64]{0:T(128)S(1)} %dynamic-update-slice), channel_id=1, replica_groups=mesh['tm'=32,'space'=8] {'tm'}, use_global_device_ids=true, to_apply=%add | all-reduce | flops 64 | bytes 512
  344.8 1.8 multiply_convert_fusion
  346.6 7.4 %fusion.16 = bf16[1,448,1120]{2,1,0:T(8,128)(2,1)S(1)} fusion(bf16[448,2240]{1,0:T(8,128)(2,1)} %bitcast.49, bf16[1,2240,1120]{2,0,1:T(2,128)(2,1)} %all-gather.8.cloned.1.call-done), kind=kOutput, calls=%fused_computation.13 | convolution fusion | flops 2248888320 | bytes 8028160 | tf_op jit(solution)/shard_map/rn,cnh->crh/dot_general | solution.py:58
  354.0 2.2 reshape.83
  356.2 21.0 %all-gather.6.cloned.1.call-done = bf16[64,140,112]{2,1,0:T(8,128)(2,1)} async-done(((bf16[2,140,112]{2,1,0:T(8,128)(2,1)}), bf16[64,140,112]{2,1,0:T(8,128)(2,1)}) %all-gather.6.cloned.1.call-update) | async-done | bytes 2007056 | tf_op jit(solution)/shard_map/all_gather | solution.py:52
  377.2 2.2 fusion.31
  379.4 27.0 %all_gather.18 = bf16[2,1120,112]{2,0,1:T(2,128)(2,1)S(1)} all-gather(bf16[2,140,112]{2,0,1:T(2,128)(2,1)S(1)} %fusion.31), channel_id=1, replica_groups=mesh['tm'=32,'space'=8] {'space'}, dimensions={1}, use_global_device_ids=true | all-gather | bytes 564480 | tf_op jit(solution)/shard_map/all_gather | solution.py:56
  406.4 0.9 fusion.19
  407.4 0.4 fusion.21
  407.7 1.4 copy.62
  (54 shorter events, 1.1 us)
Async XLA Ops:
  6.5 117.0 %copy-start.4 = (bf16[70,140]{1,0:T(8,128)(2,1)S(1)}, bf16[70,140]{1,0:T(8,128)(2,1)}, u32[]{:S(2)}) copy-start(bf16[70,140]{1,0:T(8,128)(2,1)} %param.9) | copy-start | bytes 58804
  6.5 232.9 %all-gather.4.cloned.1.call-start = ((), (), s32[]{:S(2)}) async-start(), calls=%async_computation | async-start | bytes 10644480 | tf_op jit(solution)/shard_map/all_gather | solution.py:33
  7.4 8.3 %collective-permute-start = (bf16[2,70,140]{2,1,0:T(8,128)(2,1)S(1)}, bf16[2,70,140]{2,1,0:T(8,128)(2,1)S(1)}, u32[]{:S(2)}, u32[]{:S(2)}) collective-permute-start(bf16[2,70,140]{2,1,0:T(8,128)(2,1)S(1)} %pad_maximum_fusion), channel_id=1, source_target_pairs={{0,1},{1,2},{2,3},{3,4},{4,5},{5,6},{6,7},{7,0},{8,9},{9,10},{10,1... | collective-permute-start | bytes 117608 | tf_op jit(solution)/shard_map/ppermute | solution.py:19
  9.4 6.3 %collective-permute-start.1 = (bf16[2,70,140]{2,1,0:T(8,128)(2,1)S(1)}, bf16[2,70,140]{2,1,0:T(8,128)(2,1)S(1)}, u32[]{:S(2)}, u32[]{:S(2)}) collective-permute-start(bf16[2,70,140]{2,1,0:T(8,128)(2,1)S(1)} %pad_maximum_fusion), channel_id=1, source_target_pairs={{0,7},{1,0},{2,1},{3,2},{4,3},{5,4},{6,5},{7,6},{8,15},{9,8},{10,9... | collective-permute-start | bytes 117608 | tf_op jit(solution)/shard_map/ppermute | solution.py:24
  15.6 5.6 %collective-permute-start.2 = (bf16[2,70,140]{2,1,0:T(8,128)(2,1)S(1)}, bf16[2,70,140]{2,1,0:T(8,128)(2,1)S(1)}, u32[]{:S(2)}, u32[]{:S(2)}) collective-permute-start(bf16[2,70,140]{2,1,0:T(8,128)(2,1)S(1)} %collective-permute-done), channel_id=1, source_target_pairs={{0,1},{1,2},{2,3},{3,4},{4,5},{5,6},{6,7},{7,0},{8,9},{9,10},{10,1... | collective-permute-start | bytes 117608 | tf_op jit(solution)/shard_map/ppermute | solution.py:19
  15.6 5.6 %collective-permute-start.3 = (bf16[2,70,140]{2,1,0:T(8,128)(2,1)S(1)}, bf16[2,70,140]{2,1,0:T(8,128)(2,1)S(1)}, u32[]{:S(2)}, u32[]{:S(2)}) collective-permute-start(bf16[2,70,140]{2,1,0:T(8,128)(2,1)S(1)} %collective-permute-done.1), channel_id=1, source_target_pairs={{0,7},{1,0},{2,1},{3,2},{4,3},{5,4},{6,5},{7,6},{8,15},{9,8},{10,9... | collective-permute-start | bytes 117608 | tf_op jit(solution)/shard_map/ppermute | solution.py:24
  21.2 5.6 %collective-permute-start.4 = (bf16[2,70,140]{2,1,0:T(8,128)(2,1)S(1)}, bf16[2,70,140]{2,1,0:T(8,128)(2,1)S(1)}, u32[]{:S(2)}, u32[]{:S(2)}) collective-permute-start(bf16[2,70,140]{2,1,0:T(8,128)(2,1)S(1)} %collective-permute-done.2), channel_id=1, source_target_pairs={{0,1},{1,2},{2,3},{3,4},{4,5},{5,6},{6,7},{7,0},{8,9},{9,10},{10,1... | collective-permute-start | bytes 117608 | tf_op jit(solution)/shard_map/ppermute | solution.py:19
  21.2 75.5 %collective-permute-start.5 = (bf16[2,70,140]{2,1,0:T(8,128)(2,1)S(1)}, bf16[2,70,140]{2,1,0:T(8,128)(2,1)S(1)}, u32[]{:S(2)}, u32[]{:S(2)}) collective-permute-start(bf16[2,70,140]{2,1,0:T(8,128)(2,1)S(1)} %collective-permute-done.3), channel_id=1, source_target_pairs={{0,7},{1,0},{2,1},{3,2},{4,3},{5,4},{6,5},{7,6},{8,15},{9,8},{10,9... | collective-permute-start | bytes 117608 | tf_op jit(solution)/shard_map/ppermute | solution.py:24
  26.8 83.0 %collective-permute-start.6 = (bf16[2,70,140]{2,1,0:T(8,128)(2,1)S(1)}, bf16[2,70,140]{2,1,0:T(8,128)(2,1)S(1)}, u32[]{:S(2)}, u32[]{:S(2)}) collective-permute-start(bf16[2,70,140]{2,1,0:T(8,128)(2,1)S(1)} %collective-permute-done.4), channel_id=1, source_target_pairs={{0,1},{1,2},{2,3},{3,4},{4,5},{5,6},{6,7},{7,0},{8,9},{9,10},{10,1... | collective-permute-start | bytes 117608 | tf_op jit(solution)/shard_map/ppermute | solution.py:19
  70.6 165.1 %copy-start = (bf16[2,224,2240]{2,1,0:T(8,128)(2,1)S(1)}, bf16[2,224,2240]{2,1,0:T(8,128)(2,1)}, u32[]{:S(2)}) copy-start(bf16[2,224,2240]{2,1,0:T(8,128)(2,1)} %param.7) | copy-start | bytes 6021124
  122.8 0.7 copy-start.2
  123.5 223.1 %all-gather.8.cloned.1.call-start = ((), (), s32[]{:S(2)}) async-start(), calls=%async_computation.2 | async-start | bytes 10644480 | tf_op jit(solution)/shard_map/all_gather | solution.py:33
  123.6 5.4 %collective-permute-start.7 = (bf16[1,70,140]{2,1,0:T(8,128)(2,1)S(1)}, bf16[1,70,140]{2,1,0:T(8,128)(2,1)S(1)}, u32[]{:S(2)}, u32[]{:S(2)}) collective-permute-start(bf16[1,70,140]{2,1,0:T(8,128)(2,1)S(1)} %bitcast.50), channel_id=1, source_target_pairs={{0,1},{1,2},{2,3},{3,4},{4,5},{5,6},{6,7},{7,0},{8,9},{9,10},{10,1... | collective-permute-start | bytes 58808 | tf_op jit(solution)/shard_map/ppermute | solution.py:19
  123.7 5.3 %collective-permute-start.8 = (bf16[1,70,140]{2,1,0:T(8,128)(2,1)S(1)}, bf16[1,70,140]{2,1,0:T(8,128)(2,1)S(1)}, u32[]{:S(2)}, u32[]{:S(2)}) collective-permute-start(bf16[1,70,140]{2,1,0:T(8,128)(2,1)S(1)} %bitcast.51), channel_id=1, source_target_pairs={{0,7},{1,0},{2,1},{3,2},{4,3},{5,4},{6,5},{7,6},{8,15},{9,8},{10,9... | collective-permute-start | bytes 58808 | tf_op jit(solution)/shard_map/ppermute | solution.py:24
  128.9 5.2 %collective-permute-start.9 = (bf16[1,70,140]{2,1,0:T(8,128)(2,1)S(1)}, bf16[1,70,140]{2,1,0:T(8,128)(2,1)S(1)}, u32[]{:S(2)}, u32[]{:S(2)}) collective-permute-start(bf16[1,70,140]{2,1,0:T(8,128)(2,1)S(1)} %collective-permute-done.7), channel_id=1, source_target_pairs={{0,1},{1,2},{2,3},{3,4},{4,5},{5,6},{6,7},{7,0},{8,9},{9,10},{10,1... | collective-permute-start | bytes 58808 | tf_op jit(solution)/shard_map/ppermute | solution.py:19
  128.9 5.2 %collective-permute-start.10 = (bf16[1,70,140]{2,1,0:T(8,128)(2,1)S(1)}, bf16[1,70,140]{2,1,0:T(8,128)(2,1)S(1)}, u32[]{:S(2)}, u32[]{:S(2)}) collective-permute-start(bf16[1,70,140]{2,1,0:T(8,128)(2,1)S(1)} %collective-permute-done.8), channel_id=1, source_target_pairs={{0,7},{1,0},{2,1},{3,2},{4,3},{5,4},{6,5},{7,6},{8,15},{9,8},{10,9... | collective-permute-start | bytes 58808 | tf_op jit(solution)/shard_map/ppermute | solution.py:24
  134.1 5.2 %collective-permute-start.11 = (bf16[1,70,140]{2,1,0:T(8,128)(2,1)S(1)}, bf16[1,70,140]{2,1,0:T(8,128)(2,1)S(1)}, u32[]{:S(2)}, u32[]{:S(2)}) collective-permute-start(bf16[1,70,140]{2,1,0:T(8,128)(2,1)S(1)} %collective-permute-done.9), channel_id=1, source_target_pairs={{0,1},{1,2},{2,3},{3,4},{4,5},{5,6},{6,7},{7,0},{8,9},{9,10},{10,1... | collective-permute-start | bytes 58808 | tf_op jit(solution)/shard_map/ppermute | solution.py:19
  134.1 74.4 %collective-permute-start.12 = (bf16[1,70,140]{2,1,0:T(8,128)(2,1)S(1)}, bf16[1,70,140]{2,1,0:T(8,128)(2,1)S(1)}, u32[]{:S(2)}, u32[]{:S(2)}) collective-permute-start(bf16[1,70,140]{2,1,0:T(8,128)(2,1)S(1)} %collective-permute-done.10), channel_id=1, source_target_pairs={{0,7},{1,0},{2,1},{3,2},{4,3},{5,4},{6,5},{7,6},{8,15},{9,8},{10,9... | collective-permute-start | bytes 58808 | tf_op jit(solution)/shard_map/ppermute | solution.py:24
  139.3 82.3 %collective-permute-start.13 = (bf16[1,70,140]{2,1,0:T(8,128)(2,1)S(1)}, bf16[1,70,140]{2,1,0:T(8,128)(2,1)S(1)}, u32[]{:S(2)}, u32[]{:S(2)}) collective-permute-start(bf16[1,70,140]{2,1,0:T(8,128)(2,1)S(1)} %collective-permute-done.11), channel_id=1, source_target_pairs={{0,1},{1,2},{2,3},{3,4},{4,5},{5,6},{6,7},{7,0},{8,9},{9,10},{10,1... | collective-permute-start | bytes 58808 | tf_op jit(solution)/shard_map/ppermute | solution.py:19
  143.6 92.6 %copy-start.8 = (u32[256]{0:T(256)S(1)}, u32[256]{0:T(256)}, u32[]{:S(2)}) copy-start(u32[256]{0:T(256)} %constant.105) | copy-start | bytes 3076
  143.7 94.0 %copy-start.3 = (f32[2240]{0:T(1024)S(1)}, f32[2240]{0:T(1024)}, u32[]{:S(2)}) copy-start(f32[2240]{0:T(1024)} %param.8) | copy-start | bytes 26884
  234.6 0.7 copy-start.1
  235.4 141.8 %all-gather.6.cloned.1.call-start = ((), (), s32[]{:S(2)}) async-start(), calls=%async_computation.1 | async-start | bytes 2433024 | tf_op jit(solution)/shard_map/all_gather | solution.py:52
  260.4 67.7 %copy-start.5 = (f32[1120]{0:T(1024)S(1)}, f32[1120]{0:T(1024)}, u32[]{:S(2)}) copy-start(f32[1120]{0:T(1024)} %param.12) | copy-start | bytes 13444
  260.4 67.8 %copy-start.7 = (u32[256]{0:T(256)S(1)}, u32[256]{0:T(256)}, u32[]{:S(2)}) copy-start(u32[256]{0:T(256)} %constant.99) | copy-start | bytes 3076
  260.4 69.1 %copy-start.6 = (s32[2]{0:T(128)S(1)}, s32[2]{0:T(128)}, u32[]{:S(2)}) copy-start(s32[2]{0:T(128)} %param.13) | copy-start | bytes 28
Sparse Core Ops, SparseCore 0:
  123.6 63.6 all-gather.3
  235.5 63.2 all-gather.7
  328.2 48.9 all-gather.5
